TPU v7x, 32 devices: a whole 2x2x4 slice. The times are simulated.
32 devices in a mesh: scen: 8 (over y, x, core), veh: 4 (over z).
Axes of the slice: x: 2, y: 2, z: 4, core: 2. Of those that a mesh axis runs over, the one named last changes fastest.
Arguments:
- start_plan: bfloat16 [128, 3584, 128], P('scen', 'veh'), may hold values from -6 to 6
- linear_cost: bfloat16 [128, 3584, 128], P('scen', 'veh'), may hold values from -12 to 12
- price: bfloat16 [128, 3584, 128], P('scen', 'veh'), may hold values from -6 to 6
- anchor: bfloat16 [8, 3584, 128], P(None, 'veh'), may hold values from -6 to 6
- hessian: bfloat16 [128, 128, 128], P('scen'), as said below
- usage_coef: bfloat16 [3584, 128], P('veh'), may hold values from -1.5 to 1.5
- crew_limit: float32 [128, 350], P('scen'), may hold values from -48 to 48
- crew_dual: float32 [128, 350], P('scen'), may hold values from 0 to 2
- crew_row: int32 [3584], P('veh'), may hold values from 0 to 349
- bundle_of: int32 [128, 1], replicated, may hold values from 0 to 7
- scen_weight: int32 [128], replicated, may hold values from 1 to 8
Outputs:
- new_plan: bfloat16 [128, 3584, 128], P('scen', 'veh')
- new_price: bfloat16 [128, 3584, 128], P('scen', 'veh')
- bundle_mean: bfloat16 [8, 3584, 128], P('scen', 'veh')
- new_dual: float32 [128, 350], P('scen')
- gap: float32 [], replicated
Inputs may be any that keep to these rules, and one draw needn't show every extreme that they name: `bundle_of`: every bundle holds one scenario or more. `hessian`: symmetric.
All inputs are finite; a program needn't handle non-finite values.
Results may differ from a plain program's by a relative error of at most 0.0013.
The roundings to bfloat16 on the way count: a program that leaves them out, or rounds other values in their place, can miss the bound.
Values sent between devices are 32-bit elements; how exact they have to be, the bound alone decides.
A program may use at most 128 MiB of HBM per device.

v0:
```python
import jax
import jax.numpy as jnp
from jax import lax
from jax.sharding import PartitionSpec as P

ITERS = 12
penalty = 1.0
step_size = 0.02
dual_step = 0.02
highest = lax.Precision.HIGHEST


def shards(
    start_plan,
    linear_cost,
    price,
    anchor,
    hessian,
    usage_coef,
    crew_limit,
    crew_dual,
    crew_row,
    bundle_of,
    scen_weight,
):
    local_scen = start_plan.shape[0]
    bundle_count = anchor.shape[0]
    crew_count = crew_limit.shape[1]
    offset = lax.axis_index("scen") * local_scen
    all_bundles = bundle_of[:, 0]
    my_bundles = lax.dynamic_slice_in_dim(all_bundles, offset, local_scen)
    my_weights = lax.dynamic_slice_in_dim(scen_weight, offset, local_scen).astype(jnp.float32)
    bundle_ids = jnp.arange(bundle_count, dtype=jnp.int32)
    selector = (my_bundles[:, None] == bundle_ids[None, :]).astype(jnp.float32)
    anchored = jnp.einsum(
        "sb,bvi->svi", selector.astype(jnp.bfloat16), anchor, preferred_element_type=jnp.float32
    )
    linear_part = linear_cost.astype(jnp.float32) + price.astype(jnp.float32) - penalty * anchored
    coefficient = usage_coef.astype(jnp.float32)
    crew_map = (crew_row[:, None] == jnp.arange(crew_count, dtype=jnp.int32)[None, :]).astype(
        jnp.float32
    )

    def advance(index, state_pair):
        roster, multiplier = state_pair
        rounded = roster.astype(jnp.bfloat16)
        curvature = jnp.einsum("svi,sij->svj", rounded, hessian, preferred_element_type=jnp.float32)
        consumed = jnp.sum(roster * coefficient[None], axis=2)
        partial_use = jnp.dot(consumed, crew_map, precision=highest)
        usage = lax.psum(partial_use, "veh")
        updated = jnp.maximum(multiplier + dual_step * (usage - crew_limit), 0.0)
        per_vehicle = jnp.dot(multiplier, crew_map.T, precision=highest)
        gradient = (
            curvature + linear_part + penalty * roster + per_vehicle[:, :, None] * coefficient[None]
        )
        return (roster - step_size * gradient, updated)

    roster, multiplier = lax.fori_loop(
        0, ITERS, advance, (start_plan.astype(jnp.float32), crew_dual)
    )
    weighted_pick = selector * my_weights[:, None]
    every_weight = jnp.sum(
        (all_bundles[:, None] == bundle_ids[None, :]).astype(jnp.float32)
        * scen_weight.astype(jnp.float32)[:, None],
        axis=0,
    )
    owned_rows = bundle_count // lax.axis_size("scen")
    own_start = lax.axis_index("scen") * owned_rows
    partial_sums = jnp.einsum("sb,svi->bvi", weighted_pick, roster, precision=highest)
    totals = lax.psum(partial_sums, "scen")
    every_mean = totals / every_weight[:, None, None]
    own_mean = lax.dynamic_slice_in_dim(every_mean, own_start, owned_rows)
    mean_here = jnp.einsum("sb,bvi->svi", selector, every_mean, precision=highest)
    deviation = roster - mean_here
    new_price = (price.astype(jnp.float32) + penalty * deviation).astype(jnp.bfloat16)
    spread = jnp.sum(my_weights * jnp.sum(deviation * deviation, axis=(1, 2)))
    spread_total = lax.psum(spread, ("scen", "veh"))
    entries = start_plan.shape[1] * lax.axis_size("veh") * start_plan.shape[2]
    gap = jnp.sqrt(spread_total / (jnp.sum(scen_weight.astype(jnp.float32)) * entries))
    return (roster.astype(jnp.bfloat16), new_price, own_mean.astype(jnp.bfloat16), multiplier, gap)


def solution(mesh):
    return jax.shard_map(
        shards,
        mesh=mesh,
        in_specs=(
            P("scen", "veh", None),
            P("scen", "veh", None),
            P("scen", "veh", None),
            P(None, "veh", None),
            P("scen", None, None),
            P("veh", None),
            P("scen", None),
            P("scen", None),
            P("veh"),
            P(),
            P(),
        ),
        out_specs=(
            P("scen", "veh", None),
            P("scen", "veh", None),
            P("scen", "veh", None),
            P("scen", None),
            P(),
        ),
        check_vma=False,
    )
```

profile of v0, /device:TPU:0, one launch (start us, length us, event | category | flops | bytes accessed | tf_op | source)
XLA Modules:
  0.0 568.2 jit_solution(2180171724463665782)
XLA Ops:
  8.7 22.6 %fusion.12 = f32[16,896,128]{2,0,1:T(8,128)S(1)} fusion(bf16[16,896,128]{2,1,0:T(8,128)(2,1)} %param.14, bf16[16,896,128]{2,1,0:T(8,128)(2,1)} %param.15, bf16[8,896,128]{2,1,0:T(8,128)(2,1)S(1)} %copy-done, s32[16]{0:T(128)S(1)} %dynamic-slice_bitcast_fusion), kind=kOutput, calls=%fused_computation.15 | convolution fusion | flops 36700544 | bytes 16515136 | tf_op jit(solution)/shard_map/sb,bvi->svi/dot_general | solution.py:35
  40.4 364.3 %while.13 = (s32[]{:T(128)}, f32[16,896,128]{2,1,0:T(8,128)}, f32[16,350]{1,0:T(8,128)S(1)}, bf16[16,128,128]{2,1,0:T(8,128)(2,1)S(1)}, f32[16,896,128]{2,1,0:T(...) while((s32[]{:T(128)}, f32[16,896,128]{2,1,0:T(8,128)}, ...), condition=%wide.region_3.0_spmd.clone, body=%wide.region_0.0_spmd.clone.sunk | while | flops 607967616 | bytes 75257976 | solution.py:58
  47.0 5.9 %multiply_subtract_fusion.2 = f32[16,896,128]{2,1,0:T(8,128)} fusion(f32[16,896,128]{2,1,0:T(8,128)S(1)} %copy.53, f32[16,896,128]{2,1,0:T(8,128)S(1)} %copy-done.1, f32[896,128]{1,0:T(8,128)S(1)} %get-tuple-element.185, f32[16,896]{1,0:T(8,128)S(1)} %fusion.47, bf16[16,128,128]{2,1,0:T(8,128)(2,1)S(1)} %get-tuple-element.183), kind=kOutput, calls=%fused_computation.2.clone.1 | convolution fusion | flops 482607104 | bytes 23060480 | tf_op jit(solution)/shard_map/while/body/eval_jaxpr/svi,sij->svj/dot_general | solution.py:47
  53.8 20.8 %psum.25 = f32[16,350]{1,0:T(8,128)S(1)} all-reduce(f32[16,350]{1,0:T(8,128)S(1)} %fusion.48), channel_id=1, replica_groups=mesh['scen'=8,'veh'=4] {'veh'}, use_global_device_ids=true, to_apply=%region_2.0 | all-reduce | flops 5600 | bytes 44800 | tf_op jit(solution)/shard_map/while/body/eval_jaxpr/psum | solution.py:50
  81.1 5.9 %multiply_subtract_fusion.2 = f32[16,896,128]{2,1,0:T(8,128)} fusion(f32[16,896,128]{2,1,0:T(8,128)S(1)} %copy.53, f32[16,896,128]{2,1,0:T(8,128)S(1)} %copy-done.1, f32[896,128]{1,0:T(8,128)S(1)} %get-tuple-element.185, f32[16,896]{1,0:T(8,128)S(1)} %fusion.47, bf16[16,128,128]{2,1,0:T(8,128)(2,1)S(1)} %get-tuple-element.183), kind=kOutput, calls=%fused_computation.2.clone.1 | convolution fusion | flops 482607104 | bytes 23060480 | tf_op jit(solution)/shard_map/while/body/eval_jaxpr/svi,sij->svj/dot_general | solution.py:47
  88.0 15.8 %psum.25 = f32[16,350]{1,0:T(8,128)S(1)} all-reduce(f32[16,350]{1,0:T(8,128)S(1)} %fusion.48), channel_id=1, replica_groups=mesh['scen'=8,'veh'=4] {'veh'}, use_global_device_ids=true, to_apply=%region_2.0 | all-reduce | flops 5600 | bytes 44800 | tf_op jit(solution)/shard_map/while/body/eval_jaxpr/psum | solution.py:50
  117.2 17.4 %psum.25 = f32[16,350]{1,0:T(8,128)S(1)} all-reduce(f32[16,350]{1,0:T(8,128)S(1)} %fusion.48), channel_id=1, replica_groups=mesh['scen'=8,'veh'=4] {'veh'}, use_global_device_ids=true, to_apply=%region_2.0 | all-reduce | flops 5600 | bytes 44800 | tf_op jit(solution)/shard_map/while/body/eval_jaxpr/psum | solution.py:50
  141.2 5.9 %multiply_subtract_fusion.2 = f32[16,896,128]{2,1,0:T(8,128)} fusion(f32[16,896,128]{2,1,0:T(8,128)S(1)} %copy.53, f32[16,896,128]{2,1,0:T(8,128)S(1)} %copy-done.1, f32[896,128]{1,0:T(8,128)S(1)} %get-tuple-element.185, f32[16,896]{1,0:T(8,128)S(1)} %fusion.47, bf16[16,128,128]{2,1,0:T(8,128)(2,1)S(1)} %get-tuple-element.183), kind=kOutput, calls=%fused_computation.2.clone.1 | convolution fusion | flops 482607104 | bytes 23060480 | tf_op jit(solution)/shard_map/while/body/eval_jaxpr/svi,sij->svj/dot_general | solution.py:47
  148.1 15.8 %psum.25 = f32[16,350]{1,0:T(8,128)S(1)} all-reduce(f32[16,350]{1,0:T(8,128)S(1)} %fusion.48), channel_id=1, replica_groups=mesh['scen'=8,'veh'=4] {'veh'}, use_global_device_ids=true, to_apply=%region_2.0 | all-reduce | flops 5600 | bytes 44800 | tf_op jit(solution)/shard_map/while/body/eval_jaxpr/psum | solution.py:50
  170.5 5.9 %multiply_subtract_fusion.2 = f32[16,896,128]{2,1,0:T(8,128)} fusion(f32[16,896,128]{2,1,0:T(8,128)S(1)} %copy.53, f32[16,896,128]{2,1,0:T(8,128)S(1)} %copy-done.1, f32[896,128]{1,0:T(8,128)S(1)} %get-tuple-element.185, f32[16,896]{1,0:T(8,128)S(1)} %fusion.47, bf16[16,128,128]{2,1,0:T(8,128)(2,1)S(1)} %get-tuple-element.183), kind=kOutput, calls=%fused_computation.2.clone.1 | convolution fusion | flops 482607104 | bytes 23060480 | tf_op jit(solution)/shard_map/while/body/eval_jaxpr/svi,sij->svj/dot_general | solution.py:47
  177.3 17.4 %psum.25 = f32[16,350]{1,0:T(8,128)S(1)} all-reduce(f32[16,350]{1,0:T(8,128)S(1)} %fusion.48), channel_id=1, replica_groups=mesh['scen'=8,'veh'=4] {'veh'}, use_global_device_ids=true, to_apply=%region_2.0 | all-reduce | flops 5600 | bytes 44800 | tf_op jit(solution)/shard_map/while/body/eval_jaxpr/psum | solution.py:50
  208.2 16.0 %psum.25 = f32[16,350]{1,0:T(8,128)S(1)} all-reduce(f32[16,350]{1,0:T(8,128)S(1)} %fusion.48), channel_id=1, replica_groups=mesh['scen'=8,'veh'=4] {'veh'}, use_global_device_ids=true, to_apply=%region_2.0 | all-reduce | flops 5600 | bytes 44800 | tf_op jit(solution)/shard_map/while/body/eval_jaxpr/psum | solution.py:50
  230.7 5.9 %multiply_subtract_fusion.2 = f32[16,896,128]{2,1,0:T(8,128)} fusion(f32[16,896,128]{2,1,0:T(8,128)S(1)} %copy.53, f32[16,896,128]{2,1,0:T(8,128)S(1)} %copy-done.1, f32[896,128]{1,0:T(8,128)S(1)} %get-tuple-element.185, f32[16,896]{1,0:T(8,128)S(1)} %fusion.47, bf16[16,128,128]{2,1,0:T(8,128)(2,1)S(1)} %get-tuple-element.183), kind=kOutput, calls=%fused_computation.2.clone.1 | convolution fusion | flops 482607104 | bytes 23060480 | tf_op jit(solution)/shard_map/while/body/eval_jaxpr/svi,sij->svj/dot_general | solution.py:47
  237.5 17.3 %psum.25 = f32[16,350]{1,0:T(8,128)S(1)} all-reduce(f32[16,350]{1,0:T(8,128)S(1)} %fusion.48), channel_id=1, replica_groups=mesh['scen'=8,'veh'=4] {'veh'}, use_global_device_ids=true, to_apply=%region_2.0 | all-reduce | flops 5600 | bytes 44800 | tf_op jit(solution)/shard_map/while/body/eval_jaxpr/psum | solution.py:50
  261.4 5.9 %multiply_subtract_fusion.2 = f32[16,896,128]{2,1,0:T(8,128)} fusion(f32[16,896,128]{2,1,0:T(8,128)S(1)} %copy.53, f32[16,896,128]{2,1,0:T(8,128)S(1)} %copy-done.1, f32[896,128]{1,0:T(8,128)S(1)} %get-tuple-element.185, f32[16,896]{1,0:T(8,128)S(1)} %fusion.47, bf16[16,128,128]{2,1,0:T(8,128)(2,1)S(1)} %get-tuple-element.183), kind=kOutput, calls=%fused_computation.2.clone.1 | convolution fusion | flops 482607104 | bytes 23060480 | tf_op jit(solution)/shard_map/while/body/eval_jaxpr/svi,sij->svj/dot_general | solution.py:47
  268.3 16.1 %psum.25 = f32[16,350]{1,0:T(8,128)S(1)} all-reduce(f32[16,350]{1,0:T(8,128)S(1)} %fusion.48), channel_id=1, replica_groups=mesh['scen'=8,'veh'=4] {'veh'}, use_global_device_ids=true, to_apply=%region_2.0 | all-reduce | flops 5600 | bytes 44800 | tf_op jit(solution)/shard_map/while/body/eval_jaxpr/psum | solution.py:50
  297.8 17.1 %psum.25 = f32[16,350]{1,0:T(8,128)S(1)} all-reduce(f32[16,350]{1,0:T(8,128)S(1)} %fusion.48), channel_id=1, replica_groups=mesh['scen'=8,'veh'=4] {'veh'}, use_global_device_ids=true, to_apply=%region_2.0 | all-reduce | flops 5600 | bytes 44800 | tf_op jit(solution)/shard_map/while/body/eval_jaxpr/psum | solution.py:50
  328.4 16.2 %psum.25 = f32[16,350]{1,0:T(8,128)S(1)} all-reduce(f32[16,350]{1,0:T(8,128)S(1)} %fusion.48), channel_id=1, replica_groups=mesh['scen'=8,'veh'=4] {'veh'}, use_global_device_ids=true, to_apply=%region_2.0 | all-reduce | flops 5600 | bytes 44800 | tf_op jit(solution)/shard_map/while/body/eval_jaxpr/psum | solution.py:50
  358.0 17.1 %psum.25 = f32[16,350]{1,0:T(8,128)S(1)} all-reduce(f32[16,350]{1,0:T(8,128)S(1)} %fusion.48), channel_id=1, replica_groups=mesh['scen'=8,'veh'=4] {'veh'}, use_global_device_ids=true, to_apply=%region_2.0 | all-reduce | flops 5600 | bytes 44800 | tf_op jit(solution)/shard_map/while/body/eval_jaxpr/psum | solution.py:50
  388.5 16.2 %psum.25 = f32[16,350]{1,0:T(8,128)S(1)} all-reduce(f32[16,350]{1,0:T(8,128)S(1)} %fusion.48), channel_id=1, replica_groups=mesh['scen'=8,'veh'=4] {'veh'}, use_global_device_ids=true, to_apply=%region_2.0 | all-reduce | flops 5600 | bytes 44800 | tf_op jit(solution)/shard_map/while/body/eval_jaxpr/psum | solution.py:50
  404.8 14.0 %fusion.14 = f32[8,896,128]{2,0,1:T(8,128)} fusion(f32[16,896,128]{2,1,0:T(8,128)} %get-tuple-element.48, f32[16]{0:T(128)S(1)} %dynamic-slice_convert_fusion.1, s32[16]{0:T(128)S(1)} %dynamic-slice_bitcast_fusion), kind=kOutput, calls=%fused_computation.18 | convolution fusion | flops 176161024 | bytes 11010176 | tf_op jit(solution)/shard_map/sb,svi->bvi/dot_general | solution.py:69
  425.8 67.3 %all-reduce.2.cloned.1.call-done = f32[8,896,128]{2,0,1:T(8,128)} async-done(((f32[8,896,128]{2,0,1:T(8,128)}), f32[8,896,128]{2,0,1:T(8,128)}) %all-reduce.2.cloned.1.call-update) | async-done | bytes 3670032 | tf_op jit(solution)/shard_map/psum | solution.py:70
  496.2 17.2 %multiply_reduce_fusion.1 = (f32[16]{0:T(128)S(1)}, bf16[16,896,128]{2,0,1:T(8,128)(2,1)S(1)}) fusion(bf16[16,896,128]{2,1,0:T(8,128)(2,1)S(1)} %copy-done.3, f32[8,896,128]{2,0,1:T(8,128)S(1)} %broadcast_divide_fusion, s32[16]{0:T(128)S(1)} %dynamic-slice_bitcast_fusion, f32[16,896,128]{2,1,0:T(8,128)} %get-tuple-element.48), kind=kOutput, calls=%fused_computation.17 | convolution fusion | flops 187170928 | bytes 18350208 | tf_op jit(solution)/shard_map/sb,bvi->svi/dot_general | solution.py:73
  516.9 39.5 %psum.22 = f32[]{:T(128)} all-reduce(f32[]{:T(128)} %multiply_reduce_fusion.2), channel_id=1, replica_groups=mesh['scen'=8,'veh'=4] {'scen','veh'}, use_global_device_ids=true, to_apply=%region_8.0 | all-reduce | flops 1 | bytes 8 | tf_op jit(solution)/shard_map/psum | solution.py:77
  (130 shorter events, 152.1 us)
Async XLA Ops:
  7.2 485.9 %all-reduce.2.cloned.1.call-start = ((), (), s32[]{:S(2)}) async-start(), calls=%async_computation | async-start | bytes 7340032 | tf_op jit(solution)/shard_map/psum | solution.py:70
  31.3 5.2 copy-start.5
  36.5 3.8 copy-start.9
  36.5 3.8 copy-start.4
  36.5 3.9 copy-start.7
  36.5 3.9 copy-start.8
  36.5 3.9 copy-start.11
  40.4 364.3 %copy-start.10 = (s32[128]{0:T(128)S(1)}, s32[128]{0:T(128)}, u32[]{:S(2)}) copy-start(s32[128]{0:T(128)} %param.23) | copy-start | bytes 1540
  43.5 3.5 copy-start.1
  77.7 3.5 copy-start.1
  106.9 3.5 copy-start.1
  137.8 3.5 copy-start.1
  167.0 3.5 copy-start.1
  197.9 3.5 copy-start.1
  227.2 3.5 copy-start.1
  258.0 3.5 copy-start.1
  287.5 3.5 copy-start.1
  318.1 3.5 copy-start.1
  347.7 3.5 copy-start.1
  378.1 3.5 copy-start.1
  404.7 14.1 %copy-start.6 = (f32[16,350]{1,0:T(8,128)}, f32[16,350]{1,0:T(8,128)S(1)}, u32[]{:S(2)}) copy-start(f32[16,350]{1,0:T(8,128)S(1)} %get-tuple-element.93) | copy-start | bytes 67204
  418.7 6.9 %copy-start.12 = (s32[128,1]{0,1:T(1,128)S(1)}, s32[128,1]{0,1:T(1,128)}, u32[]{:S(2)}) copy-start(s32[128,1]{0,1:T(1,128)} %param.22) | copy-start | bytes 1540
  493.1 3.1 copy-start.3
  496.2 17.2 %copy-start.2 = (f32[8,896,128]{2,0,1:T(8,128)}, f32[8,896,128]{2,0,1:T(8,128)S(1)}, u32[]{:S(2)}) copy-start(f32[8,896,128]{2,0,1:T(8,128)S(1)} %broadcast_divide_fusion) | copy-start | bytes 11010052
  (1 other events, 1.5 us)
Sparse Core Ops, SparseCore 0:
  418.9 74.1 all-reduce.1
where the time goes:
time: 569 us; the launch traced here: 568 us
  blocking collectives  243 us (43%)
  matrix products  152 us (27%)
  waiting for transfers between devices  67.3 us (12%)
  local copies, waits for them, and re-layouts  50.3 us (9%)
  other arithmetic  38.6 us (7%)
  between operations  16.7 us (3%)
    psum x12, blocking collectives, advance(): usage = lax.psum(partial_use, 'veh')  203 us
    dot_general x12, matrix products, advance(): jnp.einsum('svi,sij->svj', rounded, hessian, preferred_element_type=jnp.f...  70.6 us
    psum x1, waiting for transfers between devices, shards(): totals = lax.psum(partial_sums, 'scen')  67.3 us
    psum x1, blocking collectives, shards(): spread_total = lax.psum(spread, ('scen', 'veh'))  39.5 us
    while x36, local copies, waits for them, and re-layouts  37.1 us
    reduce_sum x12, other arithmetic, advance(): consumed = jnp.sum(roster * coefficient[None], axis=2)  25.1 us
    dot_general x1, matrix products, shards(): jnp.einsum('sb,bvi->svi', selector.astype(jnp.bfloat16), anchor, preferre...  22.6 us
    dot_general x1, matrix products, shards(): jnp.einsum('sb,bvi->svi', selector, every_mean, precision=highest)  17.2 us
  transfers between devices with their start and end apart: 1, of which 1 were waited for; matrix products, arithmetic and copies ran while one was open for 1% of the time, Pallas kernels for 0%

commit v1 on v0

--- a/solution.py
+++ b/solution.py
@@ -47,7 +47,9 @@
         curvature = jnp.einsum("svi,sij->svj", rounded, hessian, preferred_element_type=jnp.float32)
         consumed = jnp.sum(roster * coefficient[None], axis=2)
         partial_use = jnp.dot(consumed, crew_map, precision=highest)
-        usage = lax.psum(partial_use, "veh")
+        usage = partial_use
+        for hop in (1, 2):
+            usage = usage + lax.ppermute(usage, "veh", [(dev, dev ^ hop) for dev in range(4)])
         updated = jnp.maximum(multiplier + dual_step * (usage - crew_limit), 0.0)
         per_vehicle = jnp.dot(multiplier, crew_map.T, precision=highest)
         gradient = (

time: 569 us -> 417 us (0.73)
  blocking collectives: 243 us -> 39.5 us
  starting transfers between devices: 0.04 us -> 40 us
  waiting for transfers between devices: 67.3 us -> 78.8 us
    psum x12 -> x0, blocking collectives: 203 us -> none  [advance(): usage = lax.psum(partial_use, 'veh')]
    ppermute x0 -> x24, starting transfers between devices: none -> 40 us  [advance(): lax.ppermute(usage, 'veh', [(dev, dev ^ hop) for dev in range(4)])]
    ppermute x0 -> x24, waiting for transfers between devices: none -> 9.2 us  [advance(): lax.ppermute(usage, 'veh', [(dev, dev ^ hop) for dev in range(4)])]
  transfers between devices with their start and end apart: 1 -> 25, of which waited for: 1 -> 13; matrix products, arithmetic and copies ran while one was open for 1% -> 22% of each run, Pallas kernels for 0% -> 0%
where the time goes in v1:
time: 417 us; the launch traced here: 416 us
  matrix products  152 us (36%)
  waiting for transfers between devices  78.8 us (19%)
  local copies, waits for them, and re-layouts  50.3 us (12%)
  starting transfers between devices  40 us (10%)
  blocking collectives  39.5 us (9%)
  other arithmetic  38.6 us (9%)
  between operations  16.7 us (4%)
    dot_general x12, matrix products, advance(): jnp.einsum('svi,sij->svj', rounded, hessian, preferred_element_type=jnp.f...  70.3 us
    psum x1, waiting for transfers between devices, shards(): totals = lax.psum(partial_sums, 'scen')  69.6 us
    ppermute x24, starting transfers between devices, advance(): lax.ppermute(usage, 'veh', [(dev, dev ^ hop) for dev in range(4)])  40 us
    psum x1, blocking collectives, shards(): spread_total = lax.psum(spread, ('scen', 'veh'))  39.5 us
    while x36, local copies, waits for them, and re-layouts  37.1 us
    reduce_sum x12, other arithmetic, advance(): consumed = jnp.sum(roster * coefficient[None], axis=2)  25.1 us
    dot_general x1, matrix products, shards(): jnp.einsum('sb,bvi->svi', selector.astype(jnp.bfloat16), anchor, preferre...  22.6 us
    dot_general x1, matrix products, shards(): jnp.einsum('sb,bvi->svi', selector, every_mean, precision=highest)  17.2 us
  transfers between devices with their start and end apart: 25, of which 13 were waited for; matrix products, arithmetic and copies ran while one was open for 22% of the time, Pallas kernels for 0%

profile of v1, /device:TPU:0, one launch (start us, length us, event | category | flops | bytes accessed | tf_op | source)
XLA Modules:
  0.0 416.3 jit_solution(16136138179437869728)
XLA Ops:
  8.7 22.6 %fusion.12 = f32[16,896,128]{2,0,1:T(8,128)S(1)} fusion(bf16[16,896,128]{2,1,0:T(8,128)(2,1)} %param.14, bf16[16,896,128]{2,1,0:T(8,128)(2,1)} %param.15, bf16[8,896,128]{2,1,0:T(8,128)(2,1)S(1)} %copy-done, s32[16]{0:T(128)S(1)} %dynamic-slice_bitcast_fusion), kind=kOutput, calls=%fused_computation.15 | convolution fusion | flops 36700544 | bytes 16515136 | tf_op jit(solution)/shard_map/sb,bvi->svi/dot_general | solution.py:35
  31.3 5.2 %copy.27 = f32[16,896,128]{2,1,0:T(8,128)} copy(f32[16,896,128]{2,0,1:T(8,128)S(1)} %fusion.12) | data formatting | bytes 14680064
  36.5 3.8 convert_element_type.42
  40.4 210.0 %while.13 = (s32[]{:T(128)}, f32[16,896,128]{2,1,0:T(8,128)}, f32[16,350]{1,0:T(8,128)S(1)}, bf16[16,128,128]{2,1,0:T(8,128)(2,1)S(1)}, f32[16,896,128]{2,1,0:T(...) while((s32[]{:T(128)}, f32[16,896,128]{2,1,0:T(8,128)}, ...), condition=%wide.region_2.0_spmd.clone, body=%wide.region_0.0_spmd.clone.sunk | while | flops 607973248 | bytes 75482056 | solution.py:60
  40.5 3.1 copy.53
  46.6 3.1 collective-permute-start
  54.6 5.9 %multiply_subtract_fusion.2 = f32[16,896,128]{2,1,0:T(8,128)} fusion(f32[16,896,128]{2,1,0:T(8,128)S(1)} %copy.53, f32[16,896,128]{2,1,0:T(8,128)S(1)} %copy-done.1, f32[896,128]{1,0:T(8,128)S(1)} %get-tuple-element.185, f32[16,896]{1,0:T(8,128)S(1)} %fusion.47, bf16[16,128,128]{2,1,0:T(8,128)(2,1)S(1)} %get-tuple-element.183), kind=kOutput, calls=%fused_computation.2.clone.1 | convolution fusion | flops 482607104 | bytes 23060480 | tf_op jit(solution)/shard_map/while/body/eval_jaxpr/svi,sij->svj/dot_general | solution.py:47
  60.4 3.1 copy.53
  70.5 5.9 %multiply_subtract_fusion.2 = f32[16,896,128]{2,1,0:T(8,128)} fusion(f32[16,896,128]{2,1,0:T(8,128)S(1)} %copy.53, f32[16,896,128]{2,1,0:T(8,128)S(1)} %copy-done.1, f32[896,128]{1,0:T(8,128)S(1)} %get-tuple-element.185, f32[16,896]{1,0:T(8,128)S(1)} %fusion.47, bf16[16,128,128]{2,1,0:T(8,128)(2,1)S(1)} %get-tuple-element.183), kind=kOutput, calls=%fused_computation.2.clone.1 | convolution fusion | flops 482607104 | bytes 23060480 | tf_op jit(solution)/shard_map/while/body/eval_jaxpr/svi,sij->svj/dot_general | solution.py:47
  89.3 5.9 %multiply_subtract_fusion.2 = f32[16,896,128]{2,1,0:T(8,128)} fusion(f32[16,896,128]{2,1,0:T(8,128)S(1)} %copy.53, f32[16,896,128]{2,1,0:T(8,128)S(1)} %copy-done.1, f32[896,128]{1,0:T(8,128)S(1)} %get-tuple-element.185, f32[16,896]{1,0:T(8,128)S(1)} %fusion.47, bf16[16,128,128]{2,1,0:T(8,128)(2,1)S(1)} %get-tuple-element.183), kind=kOutput, calls=%fused_computation.2.clone.1 | convolution fusion | flops 482607104 | bytes 23060480 | tf_op jit(solution)/shard_map/while/body/eval_jaxpr/svi,sij->svj/dot_general | solution.py:47
  105.5 5.9 %multiply_subtract_fusion.2 = f32[16,896,128]{2,1,0:T(8,128)} fusion(f32[16,896,128]{2,1,0:T(8,128)S(1)} %copy.53, f32[16,896,128]{2,1,0:T(8,128)S(1)} %copy-done.1, f32[896,128]{1,0:T(8,128)S(1)} %get-tuple-element.185, f32[16,896]{1,0:T(8,128)S(1)} %fusion.47, bf16[16,128,128]{2,1,0:T(8,128)(2,1)S(1)} %get-tuple-element.183), kind=kOutput, calls=%fused_computation.2.clone.1 | convolution fusion | flops 482607104 | bytes 23060480 | tf_op jit(solution)/shard_map/while/body/eval_jaxpr/svi,sij->svj/dot_general | solution.py:47
  124.1 5.9 %multiply_subtract_fusion.2 = f32[16,896,128]{2,1,0:T(8,128)} fusion(f32[16,896,128]{2,1,0:T(8,128)S(1)} %copy.53, f32[16,896,128]{2,1,0:T(8,128)S(1)} %copy-done.1, f32[896,128]{1,0:T(8,128)S(1)} %get-tuple-element.185, f32[16,896]{1,0:T(8,128)S(1)} %fusion.47, bf16[16,128,128]{2,1,0:T(8,128)(2,1)S(1)} %get-tuple-element.183), kind=kOutput, calls=%fused_computation.2.clone.1 | convolution fusion | flops 482607104 | bytes 23060480 | tf_op jit(solution)/shard_map/while/body/eval_jaxpr/svi,sij->svj/dot_general | solution.py:47
  140.3 5.9 %multiply_subtract_fusion.2 = f32[16,896,128]{2,1,0:T(8,128)} fusion(f32[16,896,128]{2,1,0:T(8,128)S(1)} %copy.53, f32[16,896,128]{2,1,0:T(8,128)S(1)} %copy-done.1, f32[896,128]{1,0:T(8,128)S(1)} %get-tuple-element.185, f32[16,896]{1,0:T(8,128)S(1)} %fusion.47, bf16[16,128,128]{2,1,0:T(8,128)(2,1)S(1)} %get-tuple-element.183), kind=kOutput, calls=%fused_computation.2.clone.1 | convolution fusion | flops 482607104 | bytes 23060480 | tf_op jit(solution)/shard_map/while/body/eval_jaxpr/svi,sij->svj/dot_general | solution.py:47
  158.9 5.9 %multiply_subtract_fusion.2 = f32[16,896,128]{2,1,0:T(8,128)} fusion(f32[16,896,128]{2,1,0:T(8,128)S(1)} %copy.53, f32[16,896,128]{2,1,0:T(8,128)S(1)} %copy-done.1, f32[896,128]{1,0:T(8,128)S(1)} %get-tuple-element.185, f32[16,896]{1,0:T(8,128)S(1)} %fusion.47, bf16[16,128,128]{2,1,0:T(8,128)(2,1)S(1)} %get-tuple-element.183), kind=kOutput, calls=%fused_computation.2.clone.1 | convolution fusion | flops 482607104 | bytes 23060480 | tf_op jit(solution)/shard_map/while/body/eval_jaxpr/svi,sij->svj/dot_general | solution.py:47
  175.1 5.9 %multiply_subtract_fusion.2 = f32[16,896,128]{2,1,0:T(8,128)} fusion(f32[16,896,128]{2,1,0:T(8,128)S(1)} %copy.53, f32[16,896,128]{2,1,0:T(8,128)S(1)} %copy-done.1, f32[896,128]{1,0:T(8,128)S(1)} %get-tuple-element.185, f32[16,896]{1,0:T(8,128)S(1)} %fusion.47, bf16[16,128,128]{2,1,0:T(8,128)(2,1)S(1)} %get-tuple-element.183), kind=kOutput, calls=%fused_computation.2.clone.1 | convolution fusion | flops 482607104 | bytes 23060480 | tf_op jit(solution)/shard_map/while/body/eval_jaxpr/svi,sij->svj/dot_general | solution.py:47
  193.6 5.9 %multiply_subtract_fusion.2 = f32[16,896,128]{2,1,0:T(8,128)} fusion(f32[16,896,128]{2,1,0:T(8,128)S(1)} %copy.53, f32[16,896,128]{2,1,0:T(8,128)S(1)} %copy-done.1, f32[896,128]{1,0:T(8,128)S(1)} %get-tuple-element.185, f32[16,896]{1,0:T(8,128)S(1)} %fusion.47, bf16[16,128,128]{2,1,0:T(8,128)(2,1)S(1)} %get-tuple-element.183), kind=kOutput, calls=%fused_computation.2.clone.1 | convolution fusion | flops 482607104 | bytes 23060480 | tf_op jit(solution)/shard_map/while/body/eval_jaxpr/svi,sij->svj/dot_general | solution.py:47
  209.8 5.9 %multiply_subtract_fusion.2 = f32[16,896,128]{2,1,0:T(8,128)} fusion(f32[16,896,128]{2,1,0:T(8,128)S(1)} %copy.53, f32[16,896,128]{2,1,0:T(8,128)S(1)} %copy-done.1, f32[896,128]{1,0:T(8,128)S(1)} %get-tuple-element.185, f32[16,896]{1,0:T(8,128)S(1)} %fusion.47, bf16[16,128,128]{2,1,0:T(8,128)(2,1)S(1)} %get-tuple-element.183), kind=kOutput, calls=%fused_computation.2.clone.1 | convolution fusion | flops 482607104 | bytes 23060480 | tf_op jit(solution)/shard_map/while/body/eval_jaxpr/svi,sij->svj/dot_general | solution.py:47
  228.5 5.9 %multiply_subtract_fusion.2 = f32[16,896,128]{2,1,0:T(8,128)} fusion(f32[16,896,128]{2,1,0:T(8,128)S(1)} %copy.53, f32[16,896,128]{2,1,0:T(8,128)S(1)} %copy-done.1, f32[896,128]{1,0:T(8,128)S(1)} %get-tuple-element.185, f32[16,896]{1,0:T(8,128)S(1)} %fusion.47, bf16[16,128,128]{2,1,0:T(8,128)(2,1)S(1)} %get-tuple-element.183), kind=kOutput, calls=%fused_computation.2.clone.1 | convolution fusion | flops 482607104 | bytes 23060480 | tf_op jit(solution)/shard_map/while/body/eval_jaxpr/svi,sij->svj/dot_general | solution.py:47
  244.6 5.9 %multiply_subtract_fusion.2 = f32[16,896,128]{2,1,0:T(8,128)} fusion(f32[16,896,128]{2,1,0:T(8,128)S(1)} %copy.53, f32[16,896,128]{2,1,0:T(8,128)S(1)} %copy-done.1, f32[896,128]{1,0:T(8,128)S(1)} %get-tuple-element.185, f32[16,896]{1,0:T(8,128)S(1)} %fusion.47, bf16[16,128,128]{2,1,0:T(8,128)(2,1)S(1)} %get-tuple-element.183), kind=kOutput, calls=%fused_computation.2.clone.1 | convolution fusion | flops 482607104 | bytes 23060480 | tf_op jit(solution)/shard_map/while/body/eval_jaxpr/svi,sij->svj/dot_general | solution.py:47
  250.5 14.0 %fusion.14 = f32[8,896,128]{2,0,1:T(8,128)} fusion(f32[16,896,128]{2,1,0:T(8,128)} %get-tuple-element.48, f32[16]{0:T(128)S(1)} %dynamic-slice_convert_fusion.1, s32[16]{0:T(128)S(1)} %dynamic-slice_bitcast_fusion), kind=kOutput, calls=%fused_computation.18 | convolution fusion | flops 176161024 | bytes 11010176 | tf_op jit(solution)/shard_map/sb,svi->bvi/dot_general | solution.py:71
  264.6 5.6 %convert_element_type.49 = bf16[16,896,128]{2,1,0:T(8,128)(2,1)} convert(f32[16,896,128]{2,1,0:T(8,128)} %get-tuple-element.48) | non-fusion elementwise | flops 1835008 | bytes 11010048 | tf_op jit(solution)/shard_map/convert_element_type | solution.py:82
  271.5 69.6 %all-reduce.2.cloned.1.call-done = f32[8,896,128]{2,0,1:T(8,128)} async-done(((f32[8,896,128]{2,0,1:T(8,128)}), f32[8,896,128]{2,0,1:T(8,128)}) %all-reduce.2.cloned.1.call-update) | async-done | bytes 3670032 | tf_op jit(solution)/shard_map/psum | solution.py:72
  344.3 17.2 %multiply_reduce_fusion.1 = (f32[16]{0:T(128)S(1)}, bf16[16,896,128]{2,0,1:T(8,128)(2,1)S(1)}) fusion(bf16[16,896,128]{2,1,0:T(8,128)(2,1)S(1)} %copy-done.3, f32[8,896,128]{2,0,1:T(8,128)S(1)} %broadcast_divide_fusion, s32[16]{0:T(128)S(1)} %dynamic-slice_bitcast_fusion, f32[16,896,128]{2,1,0:T(8,128)} %get-tuple-element.48), kind=kOutput, calls=%fused_computation.17 | convolution fusion | flops 187170928 | bytes 18350208 | tf_op jit(solution)/shard_map/sb,bvi->svi/dot_general | solution.py:75
  364.9 39.5 %psum.15 = f32[]{:T(128)} all-reduce(f32[]{:T(128)} %multiply_reduce_fusion.2), channel_id=1, replica_groups=mesh['scen'=8,'veh'=4] {'scen','veh'}, use_global_device_ids=true, to_apply=%region_7.0 | all-reduce | flops 1 | bytes 8 | tf_op jit(solution)/shard_map/psum | solution.py:79
  (178 shorter events, 142.2 us)
Async XLA Ops:
  7.2 334.0 %all-reduce.2.cloned.1.call-start = ((), (), s32[]{:S(2)}) async-start(), calls=%async_computation | async-start | bytes 7340032 | tf_op jit(solution)/shard_map/psum | solution.py:72
  46.6 4.9 %collective-permute-start = (f32[16,350]{1,0:T(8,128)S(1)}, f32[16,350]{1,0:T(8,128)S(1)}, u32[]{:S(2)}, u32[]{:S(2)}) collective-permute-start(f32[16,350]{1,0:T(8,128)S(1)} %fusion.48), channel_id=1, source_target_pairs={{0,1},{1,0},{2,3},{3,2},{4,5},{5,4},{6,7},{7,6},{8,9},{9,8},{10,11... | collective-permute-start | bytes 67208 | tf_op jit(solution)/shard_map/while/body/eval_jaxpr/ppermute | solution.py:52
  51.5 8.9 %collective-permute-start.1 = (f32[16,350]{1,0:T(8,128)S(1)}, f32[16,350]{1,0:T(8,128)S(1)}, u32[]{:S(2)}, u32[]{:S(2)}) collective-permute-start(f32[16,350]{1,0:T(8,128)S(1)} %add.73), channel_id=1, source_target_pairs={{0,2},{1,3},{2,0},{3,1},{4,6},{5,7},{6,4},{7,5},{8,10},{9,11},{10,... | collective-permute-start | bytes 67208 | tf_op jit(solution)/shard_map/while/body/eval_jaxpr/ppermute | solution.py:52
  66.6 3.9 collective-permute-start
  70.5 5.9 %collective-permute-start.1 = (f32[16,350]{1,0:T(8,128)S(1)}, f32[16,350]{1,0:T(8,128)S(1)}, u32[]{:S(2)}, u32[]{:S(2)}) collective-permute-start(f32[16,350]{1,0:T(8,128)S(1)} %add.73), channel_id=1, source_target_pairs={{0,2},{1,3},{2,0},{3,1},{4,6},{5,7},{6,4},{7,5},{8,10},{9,11},{10,... | collective-permute-start | bytes 67208 | tf_op jit(solution)/shard_map/while/body/eval_jaxpr/ppermute | solution.py:52
  82.5 4.1 collective-permute-start
  86.7 8.5 %collective-permute-start.1 = (f32[16,350]{1,0:T(8,128)S(1)}, f32[16,350]{1,0:T(8,128)S(1)}, u32[]{:S(2)}, u32[]{:S(2)}) collective-permute-start(f32[16,350]{1,0:T(8,128)S(1)} %add.73), channel_id=1, source_target_pairs={{0,2},{1,3},{2,0},{3,1},{4,6},{5,7},{6,4},{7,5},{8,10},{9,11},{10,... | collective-permute-start | bytes 67208 | tf_op jit(solution)/shard_map/while/body/eval_jaxpr/ppermute | solution.py:52
  101.3 3.9 collective-permute-start
  105.2 6.1 %collective-permute-start.1 = (f32[16,350]{1,0:T(8,128)S(1)}, f32[16,350]{1,0:T(8,128)S(1)}, u32[]{:S(2)}, u32[]{:S(2)}) collective-permute-start(f32[16,350]{1,0:T(8,128)S(1)} %add.73), channel_id=1, source_target_pairs={{0,2},{1,3},{2,0},{3,1},{4,6},{5,7},{6,4},{7,5},{8,10},{9,11},{10,... | collective-permute-start | bytes 67208 | tf_op jit(solution)/shard_map/while/body/eval_jaxpr/ppermute | solution.py:52
  117.5 3.9 collective-permute-start
  121.4 8.5 %collective-permute-start.1 = (f32[16,350]{1,0:T(8,128)S(1)}, f32[16,350]{1,0:T(8,128)S(1)}, u32[]{:S(2)}, u32[]{:S(2)}) collective-permute-start(f32[16,350]{1,0:T(8,128)S(1)} %add.73), channel_id=1, source_target_pairs={{0,2},{1,3},{2,0},{3,1},{4,6},{5,7},{6,4},{7,5},{8,10},{9,11},{10,... | collective-permute-start | bytes 67208 | tf_op jit(solution)/shard_map/while/body/eval_jaxpr/ppermute | solution.py:52
  136.1 3.9 collective-permute-start
  140.0 6.1 %collective-permute-start.1 = (f32[16,350]{1,0:T(8,128)S(1)}, f32[16,350]{1,0:T(8,128)S(1)}, u32[]{:S(2)}, u32[]{:S(2)}) collective-permute-start(f32[16,350]{1,0:T(8,128)S(1)} %add.73), channel_id=1, source_target_pairs={{0,2},{1,3},{2,0},{3,1},{4,6},{5,7},{6,4},{7,5},{8,10},{9,11},{10,... | collective-permute-start | bytes 67208 | tf_op jit(solution)/shard_map/while/body/eval_jaxpr/ppermute | solution.py:52
  152.3 3.9 collective-permute-start
  156.2 8.5 %collective-permute-start.1 = (f32[16,350]{1,0:T(8,128)S(1)}, f32[16,350]{1,0:T(8,128)S(1)}, u32[]{:S(2)}, u32[]{:S(2)}) collective-permute-start(f32[16,350]{1,0:T(8,128)S(1)} %add.73), channel_id=1, source_target_pairs={{0,2},{1,3},{2,0},{3,1},{4,6},{5,7},{6,4},{7,5},{8,10},{9,11},{10,... | collective-permute-start | bytes 67208 | tf_op jit(solution)/shard_map/while/body/eval_jaxpr/ppermute | solution.py:52
  170.9 3.9 collective-permute-start
  174.8 6.1 %collective-permute-start.1 = (f32[16,350]{1,0:T(8,128)S(1)}, f32[16,350]{1,0:T(8,128)S(1)}, u32[]{:S(2)}, u32[]{:S(2)}) collective-permute-start(f32[16,350]{1,0:T(8,128)S(1)} %add.73), channel_id=1, source_target_pairs={{0,2},{1,3},{2,0},{3,1},{4,6},{5,7},{6,4},{7,5},{8,10},{9,11},{10,... | collective-permute-start | bytes 67208 | tf_op jit(solution)/shard_map/while/body/eval_jaxpr/ppermute | solution.py:52
  187.1 3.9 collective-permute-start
  191.0 8.5 %collective-permute-start.1 = (f32[16,350]{1,0:T(8,128)S(1)}, f32[16,350]{1,0:T(8,128)S(1)}, u32[]{:S(2)}, u32[]{:S(2)}) collective-permute-start(f32[16,350]{1,0:T(8,128)S(1)} %add.73), channel_id=1, source_target_pairs={{0,2},{1,3},{2,0},{3,1},{4,6},{5,7},{6,4},{7,5},{8,10},{9,11},{10,... | collective-permute-start | bytes 67208 | tf_op jit(solution)/shard_map/while/body/eval_jaxpr/ppermute | solution.py:52
  205.6 3.9 collective-permute-start
  209.5 6.1 %collective-permute-start.1 = (f32[16,350]{1,0:T(8,128)S(1)}, f32[16,350]{1,0:T(8,128)S(1)}, u32[]{:S(2)}, u32[]{:S(2)}) collective-permute-start(f32[16,350]{1,0:T(8,128)S(1)} %add.73), channel_id=1, source_target_pairs={{0,2},{1,3},{2,0},{3,1},{4,6},{5,7},{6,4},{7,5},{8,10},{9,11},{10,... | collective-permute-start | bytes 67208 | tf_op jit(solution)/shard_map/while/body/eval_jaxpr/ppermute | solution.py:52
  221.8 3.9 collective-permute-start
  225.7 8.6 %collective-permute-start.1 = (f32[16,350]{1,0:T(8,128)S(1)}, f32[16,350]{1,0:T(8,128)S(1)}, u32[]{:S(2)}, u32[]{:S(2)}) collective-permute-start(f32[16,350]{1,0:T(8,128)S(1)} %add.73), channel_id=1, source_target_pairs={{0,2},{1,3},{2,0},{3,1},{4,6},{5,7},{6,4},{7,5},{8,10},{9,11},{10,... | collective-permute-start | bytes 67208 | tf_op jit(solution)/shard_map/while/body/eval_jaxpr/ppermute | solution.py:52
  244.4 6.0 %collective-permute-start.1 = (f32[16,350]{1,0:T(8,128)S(1)}, f32[16,350]{1,0:T(8,128)S(1)}, u32[]{:S(2)}, u32[]{:S(2)}) collective-permute-start(f32[16,350]{1,0:T(8,128)S(1)} %add.73), channel_id=1, source_target_pairs={{0,2},{1,3},{2,0},{3,1},{4,6},{5,7},{6,4},{7,5},{8,10},{9,11},{10,... | collective-permute-start | bytes 67208 | tf_op jit(solution)/shard_map/while/body/eval_jaxpr/ppermute | solution.py:52
  (25 other events, 177.7 us)
Sparse Core Ops, SparseCore 0:
  264.7 76.4 all-reduce.1
